TPU v7x, 32 devices: a whole 2x2x4 slice. The times are simulated.
32 devices in a mesh: row: 16 (over z, y, core), col: 2 (over x).
Axes of the slice: x: 2, y: 2, z: 4, core: 2. Of those that a mesh axis runs over, the one named last changes fastest.
Arguments:
- damping: bfloat16 [1536, 128, 1536], P('col', 'row'), may hold values from -60 to 60
- block_seeds: int32 [32], replicated, may hold values from 1 to 65520
Outputs:
- basis: float32 [32, 1536, 32], P('row', 'col')
All inputs are finite; a program needn't handle non-finite values.
Results may differ from a plain program's by a relative error of at most 0.0057.
Values may be sent and summed in bfloat16 or wider, within the bound.
No kernel may reach another device: no remote copies, remote signals or barrier semaphores. Data moves between devices by JAX's collectives and lax.ppermute only.
A program may use at most 192 MiB of HBM per device.

v0:
```python
import math
import jax
import jax.numpy as jnp
from jax import lax
from jax.sharding import PartitionSpec as P

NF = 128
M = 1536
P_SIZE = 32
NB = 32
NSTEPS = 12


def lag_table():
    lag_idx = jnp.arange(2 * NB, dtype=jnp.float32)[:, None]
    freq_idx = jnp.arange(NF, dtype=jnp.float32)[None, :]
    window = jnp.exp(-math.log(3.0) * lag_idx / NB)
    cos_table = (
        jnp.cos(math.pi * (freq_idx + 0.5) * lag_idx / NF)
        * window
        * math.sqrt(2.0 / NF)
        / math.sqrt(NB * M)
    )
    return cos_table.astype(jnp.bfloat16)


def probe_blocks(block_seeds, start_col, number):
    prime_mod = 65521
    column = (start_col + jnp.arange(number, dtype=jnp.int32))[None, :, None]
    probe_col = jnp.arange(P_SIZE, dtype=jnp.int32)[None, None, :]
    seed_col = block_seeds[:, None, None]
    inner_part = seed_col * (column + 1) % prime_mod * (column + 3) % prime_mod
    phase_val = (
        inner_part * (probe_col + 1) + seed_col * (probe_col + 1) % prime_mod * (probe_col + 2)
    ) % prime_mod
    return jnp.cos(2.0 * math.pi * phase_val.astype(jnp.float32) / prime_mod).astype(jnp.bfloat16)


def hankel_stack(blocks, group_len):
    extent = blocks.shape[0] + group_len - 1
    padded = jnp.pad(blocks, ((group_len - 1, group_len - 1), (0, 0), (0, 0)))
    shifted = [
        padded[group_len - 1 - offset : group_len - 1 - offset + extent]
        for offset in range(group_len)
    ]
    return jnp.stack(shifted, axis=2).reshape(extent, blocks.shape[1], group_len * blocks.shape[2])


def hankel_pass(lag_tiles, stack, shift_by, form, group_len):
    extent = stack.shape[0]
    pieces = []
    for group in range(NB // group_len):
        start_lag = group * group_len + shift_by
        window_lags = lag_tiles[start_lag : start_lag + extent]
        product = jnp.einsum(form, window_lags, stack, preferred_element_type=jnp.float32)
        pieces.append(product.reshape(product.shape[0], group_len, P_SIZE).transpose(1, 0, 2))
    return jnp.concatenate(pieces, axis=0)


def gram_of(blocks):
    return jnp.einsum("bcp,bcq->pq", blocks, blocks, precision=lax.Precision.HIGHEST)


def finish(mine, gram):
    highest = lax.Precision.HIGHEST
    scale = jnp.trace(gram) + 1e-06
    current = gram / scale
    eye_mat = jnp.eye(P_SIZE, dtype=jnp.float32)
    inverse = eye_mat
    for repeat in range(NSTEPS):
        weight = 1.5 * eye_mat - 0.5 * jnp.dot(inverse, current, precision=highest)
        current = jnp.dot(current, weight, precision=highest)
        inverse = jnp.dot(weight, inverse, precision=highest)
    factor = math.sqrt(NB * M) / jnp.sqrt(scale)
    return factor * jnp.einsum("bcp,pq->bcq", mine, inverse, precision=highest)


def shards(damping, block_seeds):
    group_len = min(16, NB)
    tile_cols = damping.shape[0]
    cos_table = lag_table()
    lag_tiles = jnp.einsum(
        "lk,nkr->lrn",
        cos_table,
        lax.all_to_all(damping, "row", split_axis=2, concat_axis=1, tiled=True),
        preferred_element_type=jnp.float32,
    ).astype(jnp.bfloat16)
    local_probes = probe_blocks(block_seeds, lax.axis_index("col") * tile_cols, tile_cols)
    partial_rows = hankel_pass(
        lag_tiles, hankel_stack(local_probes, group_len), 0, "lrc,lcn->rn", group_len
    )
    forward_b = lax.psum(partial_rows, "col").astype(jnp.bfloat16)
    partial_cols = hankel_pass(
        lag_tiles, hankel_stack(forward_b, group_len), 1, "lrc,lrn->cn", group_len
    )
    mine = lax.psum_scatter(partial_cols, "row", scatter_dimension=0, tiled=True)
    gram = lax.psum(gram_of(mine), ("row", "col"))
    return finish(mine, gram)


def solution(mesh):
    return jax.shard_map(
        shards,
        mesh=mesh,
        in_specs=(P("col", "row", None), P()),
        out_specs=P("row", "col", None),
        check_vma=False,
    )
```

profile of v0, /device:TPU:0, one launch (start us, length us, event | category | flops | bytes accessed | tf_op | source)
XLA Modules:
  0.0 698.7 jit_solution(12683558152289276993)
XLA Ops:
  6.5 26.8 %copy.35 = bf16[768,8,1536]{0,1,2:T(8,128)(2,1)} copy(bf16[768,8,1536]{2,1,0:T(8,128)(2,1)} %param.2) | data formatting | bytes 37748736 | tf_op args[0]
  33.3 7.6 %all-to-all-start = ((bf16[768,8,1536]{0,1,2:T(8,128)(2,1)}), bf16[768,8,1536]{0,1,2:T(8,128)(2,1)}, u32[]{:S(2)}, u32[]{:S(2)}) async-start(bf16[768,8,1536]{0,1,2:T(8,128)(2,1)} %copy.35), calls=%async_computation | async-start | bytes 37748736 | tf_op jit(solution)/shard_map/all_to_all | solution.py:85
  41.3 12.4 %fusion.23 = bf16[32,768,32]{1,2,0:T(8,128)(2,1)S(1)} fusion(s32[32,32]{1,0:T(8,128)S(1)} %fusion.133, s32[32]{0:T(128)S(1)} %get-tuple-element.10, s32[32,768]{1,0:T(8,128)S(1)} %add_select_fusion.1), kind=kLoop, calls=%fused_computation.39 | loop fusion | flops 8650752 | bytes 1675392 | tf_op jit(solution)/shard_map/convert_element_type | solution.py:36
  53.7 1.7 fusion.28
  55.4 1.7 fusion.30
  57.1 1.7 fusion.32
  58.7 1.7 fusion.34
  60.4 1.7 fusion.36
  62.1 1.7 fusion.38
  63.8 1.7 fusion.40
  65.5 1.7 fusion.42
  67.2 1.7 fusion.44
  68.9 1.7 fusion.46
  70.6 1.7 fusion.48
  72.3 1.7 fusion.50
  74.0 1.7 fusion.52
  75.6 1.7 fusion.54
  77.3 1.7 fusion.56
  79.0 1.7 fusion.58
  80.7 293.4 %all-to-all-done = bf16[768,8,1536]{0,1,2:T(8,128)(2,1)} async-done(((bf16[768,8,1536]{0,1,2:T(8,128)(2,1)}), bf16[768,8,1536]{0,1,2:T(8,128)(2,1)}, u32[]{:S(2)}, u32[]{:S(2)}) %all-to-all-start) | async-done | bytes 18874400 | tf_op jit(solution)/shard_map/all_to_all | solution.py:85
  374.1 18.7 %copy.37 = bf16[768,16,8,96]{0,3,2,1:T(8,128)(2,1)} copy(bf16[768,16,8,96]{0,2,3,1:T(8,128)(2,1)} %bitcast.41) | data formatting | bytes 37748736 | tf_op jit(solution)/shard_map/all_to_all | solution.py:85
  392.8 26.2 %convert_bitcast_fusion = bf16[64,96,768]{2,0,1:T(8,128)(2,1)S(1)} fusion(bf16[768,128,96]{0,2,1:T(8,128)(2,1)} %bitcast.321, f32[64]{0:T(128)S(1)} %multiply_exponential_fusion, f32[128]{0:T(128)S(1)} %add_multiply_fusion), kind=kOutput, calls=%fused_computation.6 | convolution fusion | flops 1212719104 | bytes 28312320 | tf_op jit(solution)/shard_map/lk,nkr->lrn/dot_general | solution.py:82
  419.0 8.6 %fusion.147 = (bf16[47,96,768]{2,0,1:T(8,128)(2,1)}, bf16[47,96,768]{2,0,1:T(8,128)(2,1)}, bf16[47,96,768]{2,0,1:T(8,128)(2,1)}, bf16[47,96,768]{2,0,1:T(8,128)(2,1)S(1)}) fusion(bf16[64,96,768]{2,0,1:T(8,128)(2,1)S(1)} %convert_bitcast_fusion), kind=kLoop, calls=%fused_computation.194 | loop fusion | bytes 55443456 | tf_op jit(solution)/shard_map/slice | solution.py:54
  427.6 22.3 %fusion.69 = f32[16,96,32]{1,2,0:T(8,128)S(1)} fusion(bf16[47,768,16,32]{1,3,2,0:T(8,128)(2,1)} %fusion.58, bf16[47,96,768]{2,0,1:T(8,128)(2,1)} %get-tuple-element.7), kind=kOutput, calls=%fused_computation.95 | convolution fusion | flops 3548381184 | bytes 44089344 | tf_op jit(solution)/shard_map/lrc,lcn->rn/dot_general | solution.py:55
  449.9 15.9 %fusion.74 = f32[16,96,32]{1,2,0:T(8,128)S(1)} fusion(bf16[47,768,16,32]{1,3,2,0:T(8,128)(2,1)} %fusion.58, bf16[47,96,768]{2,0,1:T(8,128)(2,1)S(1)} %get-tuple-element.8), kind=kOutput, calls=%fused_computation.96 | convolution fusion | flops 3548381184 | bytes 44089344 | tf_op jit(solution)/shard_map/lrc,lcn->rn/dot_general | solution.py:55
  465.9 19.4 %all-reduce.3 = bf16[32,96,32]{1,2,0:T(8,128)(2,1)S(1)} all-reduce(f32[32,96,32]{1,2,0:T(8,128)S(1)} %pad_maximum_fusion.1), channel_id=1, replica_groups=mesh['row'=16,'col'=2] {'col'}, use_global_device_ids=true, to_apply=%region_0.1 | all-reduce | flops 98304 | bytes 589824 | tf_op jit(solution)/shard_map/psum | solution.py:92
  486.8 8.5 %fusion.59 = f32[16,768,32]{1,2,0:T(8,128)S(1)} fusion(bf16[47,96,16,32]{1,3,0,2:T(8,128)(2,1)S(1)} %fusion.122, bf16[47,96,768]{2,0,1:T(8,128)(2,1)} %get-tuple-element.5), kind=kOutput, calls=%fused_computation.77 | convolution fusion | flops 3548381184 | bytes 13123584 | tf_op jit(solution)/shard_map/lrc,lrn->cn/dot_general | solution.py:55
  495.3 6.2 fusion.64
  501.5 1.9 pad_maximum_fusion
  503.4 138.3 %reduce-scatter.2.cloned.1.call-done = f32[2,768,32]{1,2,0:T(8,128)} async-done(((f32[32,768,32]{1,2,0:T(8,128)}), f32[2,768,32]{1,2,0:T(8,128)}) %reduce-scatter.2.cloned.1.call-update) | async-done | bytes 196624 | tf_op jit(solution)/shard_map/reduce_scatter | solution.py:96
  643.1 39.8 %psum.15 = f32[32,32]{1,0:T(8,128)S(1)} all-reduce(f32[32,32]{1,0:T(8,128)S(1)} %convolution_bitcast_fusion.1), channel_id=1, replica_groups=mesh['row'=16,'col'=2] {'row','col'}, use_global_device_ids=true, to_apply=%region_2.3 | all-reduce | flops 1024 | bytes 8192 | tf_op jit(solution)/shard_map/psum | solution.py:97
  689.6 1.9 convolution_multiply_fusion
  (69 shorter events, 9.0 us)
Async XLA Ops:
  33.3 7.7 %copy-start = (s32[32]{0:T(128)S(1)}, s32[32]{0:T(128)}, u32[]{:S(2)}) copy-start(s32[32]{0:T(128)} %param.3) | copy-start | bytes 388
  33.3 340.8 %all-to-all-start = ((bf16[768,8,1536]{0,1,2:T(8,128)(2,1)}), bf16[768,8,1536]{0,1,2:T(8,128)(2,1)}, u32[]{:S(2)}, u32[]{:S(2)}) async-start(bf16[768,8,1536]{0,1,2:T(8,128)(2,1)} %copy.35), calls=%async_computation | async-start | bytes 37748736 | tf_op jit(solution)/shard_map/all_to_all | solution.py:85
  40.9 600.8 %reduce-scatter.2.cloned.1.call-start = ((), (), s32[]{:S(2)}) async-start(), calls=%async_computation.2 | async-start | bytes 3342336 | tf_op jit(solution)/shard_map/reduce_scatter | solution.py:96
  486.3 9.0 %slice-start = ((s8[7077888]{0:T(1024)(128)(4,1)}), s8[4194304]{0:T(1024)(128)(4,1)S(1)}, s32[]{:S(2)}) async-start(s8[7077888]{0:T(1024)(128)(4,1)} %bitcast.322), calls=%async_computation.3 | async-start | bytes 8388608
  486.8 8.5 %slice-start.1 = ((s8[7077888]{0:T(1024)(128)(4,1)}), s8[2883584]{0:T(1024)(128)(4,1)S(1)}, s32[]{:S(2)}) async-start(s8[7077888]{0:T(1024)(128)(4,1)} %bitcast.322), calls=%async_computation.4 | async-start | bytes 5767168
Sparse Core Ops, SparseCore 0:
  503.5 138.1 reduce-scatter.1
where the time goes:
time: 706 us; the launch traced here: 699 us
  waiting for transfers between devices  432 us (61%)
  matrix products  87.6 us (12%)
  local copies, waits for them, and re-layouts  82.6 us (12%)
  blocking collectives  59.2 us (8%)
  other arithmetic  15.2 us (2%)
  between operations  14.8 us (2%)
  starting transfers between devices  7.63 us (1%)
    all_to_all x1, waiting for transfers between devices, shards(): lax.all_to_all(damping, 'row', split_axis=2, concat_axis=1, tiled=True)  293 us
    reduce_scatter x1, waiting for transfers between devices, shards(): lax.psum_scatter(partial_cols, 'row', scatter_dimension=0, tiled=True)  138 us
    unnamed x37, local copies, waits for them, and re-layouts  53.5 us
    dot_general x4, matrix products, hankel_pass(): jnp.einsum(form, window_lags, stack, preferred_element_type=jnp.float32)  52.9 us
    psum x1, blocking collectives, shards(): gram = lax.psum(gram_of(mine), ('row', 'col'))  39.8 us
    dot_general x1, matrix products, shards(): jnp.einsum('lk,nkr->lrn', cos_table, lax.all_to_all(damping, 'row', split...  26.2 us
    psum x1, blocking collectives, shards(): forward_b = lax.psum(partial_rows, 'col').astype(jnp.bfloat16)  19.4 us
    all_to_all x1, local copies, waits for them, and re-layouts, shards(): lax.all_to_all(damping, 'row', split_axis=2, concat_axis=1, tiled=True)  18.7 us
  transfers between devices with their start and end apart: 2, of which 2 were waited for; matrix products, arithmetic and copies ran while one was open for 6% of the time, Pallas kernels for 0%

commit v1 on v0

--- a/solution.py
+++ b/solution.py
@@ -94,7 +94,8 @@
         lag_tiles, hankel_stack(forward_b, group_len), 1, "lrc,lrn->cn", group_len
     )
     mine = lax.psum_scatter(partial_cols, "row", scatter_dimension=0, tiled=True)
-    gram = lax.psum(gram_of(mine), ("row", "col"))
+    array_in = gram_of(mine)
+    gram = lax.all_gather(array_in, ("row", "col")).sum(axis=0)
     return finish(mine, gram)
 
 

time: 706 us -> 731 us (1.035)
  blocking collectives: 59.2 us -> 87 us
    all_gather x0 -> x1, blocking collectives: none -> 67.7 us  [shards(): gram = lax.all_gather(array_in, ('row', 'col')).sum(axis=0)]
    psum x1 -> x0, blocking collectives: 39.8 us -> none  [shards(): gram = lax.psum(gram_of(mine), ('row', 'col'))]
    dot_general x1, matrix products: 26.2 us -> 15.6 us  [shards(): jnp.einsum('lk,nkr->lrn', cos_table, lax.all_to_all(damping, 'row', split...]
    dot_general x4, matrix products: 52.9 us -> 60.9 us  [hankel_pass(): jnp.einsum(form, window_lags, stack, preferred_element_type=jnp.float32)]
  transfers between devices with their start and end apart: 2 -> 2, of which waited for: 2 -> 2; matrix products, arithmetic and copies ran while one was open for 6% -> 5% of each run, Pallas kernels for 0% -> 0%
where the time goes in v1:
time: 731 us; the launch traced here: 724 us
  waiting for transfers between devices  432 us (59%)
  blocking collectives  87 us (12%)
  matrix products  85 us (12%)
  local copies, waits for them, and re-layouts  82.6 us (11%)
  other arithmetic  15.3 us (2%)
  between operations  14.4 us (2%)
  starting transfers between devices  7.63 us (1%)
    all_to_all x1, waiting for transfers between devices, shards(): lax.all_to_all(damping, 'row', split_axis=2, concat_axis=1, tiled=True)  293 us
    reduce_scatter x1, waiting for transfers between devices, shards(): lax.psum_scatter(partial_cols, 'row', scatter_dimension=0, tiled=True)  138 us
    all_gather x1, blocking collectives, shards(): gram = lax.all_gather(array_in, ('row', 'col')).sum(axis=0)  67.7 us
    dot_general x4, matrix products, hankel_pass(): jnp.einsum(form, window_lags, stack, preferred_element_type=jnp.float32)  60.9 us
    unnamed x37, local copies, waits for them, and re-layouts  53.5 us
    psum x1, blocking collectives, shards(): forward_b = lax.psum(partial_rows, 'col').astype(jnp.bfloat16)  19.4 us
    all_to_all x1, local copies, waits for them, and re-layouts, shards(): lax.all_to_all(damping, 'row', split_axis=2, concat_axis=1, tiled=True)  18.7 us
    dot_general x1, matrix products, shards(): jnp.einsum('lk,nkr->lrn', cos_table, lax.all_to_all(damping, 'row', split...  15.6 us
  transfers between devices with their start and end apart: 2, of which 2 were waited for; matrix products, arithmetic and copies ran while one was open for 5% of the time, Pallas kernels for 0%

profile of v1, /device:TPU:0, one launch (start us, length us, event | category | flops | bytes accessed | tf_op | source)
XLA Modules:
  0.0 723.7 jit_solution(11959176674104294575)
XLA Ops:
  6.5 26.8 %copy.35 = bf16[768,8,1536]{0,1,2:T(8,128)(2,1)} copy(bf16[768,8,1536]{2,1,0:T(8,128)(2,1)} %param.2) | data formatting | bytes 37748736 | tf_op args[0]
  33.3 7.6 %all-to-all-start = ((bf16[768,8,1536]{0,1,2:T(8,128)(2,1)}), bf16[768,8,1536]{0,1,2:T(8,128)(2,1)}, u32[]{:S(2)}, u32[]{:S(2)}) async-start(bf16[768,8,1536]{0,1,2:T(8,128)(2,1)} %copy.35), calls=%async_computation | async-start | bytes 37748736 | tf_op jit(solution)/shard_map/all_to_all | solution.py:85
  41.3 12.4 %fusion.23 = bf16[32,768,32]{1,2,0:T(8,128)(2,1)S(1)} fusion(s32[32,32]{1,0:T(8,128)S(1)} %fusion.133, s32[32]{0:T(128)S(1)} %get-tuple-element.10, s32[32,768]{1,0:T(8,128)S(1)} %add_select_fusion.1), kind=kLoop, calls=%fused_computation.39 | loop fusion | flops 8650752 | bytes 1675392 | tf_op jit(solution)/shard_map/convert_element_type | solution.py:36
  53.7 1.7 fusion.28
  55.4 1.7 fusion.30
  57.1 1.7 fusion.32
  58.7 1.7 fusion.34
  60.4 1.7 fusion.36
  62.1 1.7 fusion.38
  63.8 1.7 fusion.40
  65.5 1.7 fusion.42
  67.2 1.7 fusion.44
  68.9 1.7 fusion.46
  70.6 1.7 fusion.48
  72.3 1.7 fusion.50
  74.0 1.7 fusion.52
  75.6 1.7 fusion.54
  77.3 1.7 fusion.56
  79.0 1.7 fusion.58
  80.7 293.4 %all-to-all-done = bf16[768,8,1536]{0,1,2:T(8,128)(2,1)} async-done(((bf16[768,8,1536]{0,1,2:T(8,128)(2,1)}), bf16[768,8,1536]{0,1,2:T(8,128)(2,1)}, u32[]{:S(2)}, u32[]{:S(2)}) %all-to-all-start) | async-done | bytes 18874400 | tf_op jit(solution)/shard_map/all_to_all | solution.py:85
  374.1 18.7 %copy.37 = bf16[768,16,8,96]{0,3,2,1:T(8,128)(2,1)} copy(bf16[768,16,8,96]{0,2,3,1:T(8,128)(2,1)} %bitcast.41) | data formatting | bytes 37748736 | tf_op jit(solution)/shard_map/all_to_all | solution.py:85
  392.8 15.6 %convert_bitcast_fusion = bf16[64,96,768]{2,0,1:T(8,128)(2,1)S(1)} fusion(bf16[768,128,96]{0,2,1:T(8,128)(2,1)} %bitcast.322, f32[64]{0:T(128)S(1)} %multiply_exponential_fusion, f32[128]{0:T(128)S(1)} %add_multiply_fusion), kind=kOutput, calls=%fused_computation.6 | convolution fusion | flops 1212719104 | bytes 28312320 | tf_op jit(solution)/shard_map/lk,nkr->lrn/dot_general | solution.py:82
  408.4 8.6 %fusion.147 = (bf16[47,96,768]{2,0,1:T(8,128)(2,1)}, bf16[47,96,768]{2,0,1:T(8,128)(2,1)}, bf16[47,96,768]{2,0,1:T(8,128)(2,1)}, bf16[47,96,768]{2,0,1:T(8,128)(2,1)S(1)}) fusion(bf16[64,96,768]{2,0,1:T(8,128)(2,1)S(1)} %convert_bitcast_fusion), kind=kLoop, calls=%fused_computation.194 | loop fusion | bytes 55443456 | tf_op jit(solution)/shard_map/slice | solution.py:54
  417.0 22.3 %fusion.69 = f32[16,96,32]{1,2,0:T(8,128)S(1)} fusion(bf16[47,768,16,32]{1,3,2,0:T(8,128)(2,1)} %fusion.58, bf16[47,96,768]{2,0,1:T(8,128)(2,1)} %get-tuple-element.7), kind=kOutput, calls=%fused_computation.95 | convolution fusion | flops 3548381184 | bytes 44089344 | tf_op jit(solution)/shard_map/lrc,lcn->rn/dot_general | solution.py:55
  439.3 15.9 %fusion.74 = f32[16,96,32]{1,2,0:T(8,128)S(1)} fusion(bf16[47,768,16,32]{1,3,2,0:T(8,128)(2,1)} %fusion.58, bf16[47,96,768]{2,0,1:T(8,128)(2,1)S(1)} %get-tuple-element.8), kind=kOutput, calls=%fused_computation.96 | convolution fusion | flops 3548381184 | bytes 44089344 | tf_op jit(solution)/shard_map/lrc,lcn->rn/dot_general | solution.py:55
  455.3 19.4 %all-reduce.3 = bf16[32,96,32]{1,2,0:T(8,128)(2,1)S(1)} all-reduce(f32[32,96,32]{1,2,0:T(8,128)S(1)} %pad_maximum_fusion.1), channel_id=1, replica_groups=mesh['row'=16,'col'=2] {'col'}, use_global_device_ids=true, to_apply=%region_0.1 | all-reduce | flops 98304 | bytes 589824 | tf_op jit(solution)/shard_map/psum | solution.py:92
  476.2 16.5 %fusion.59 = f32[16,768,32]{1,2,0:T(8,128)S(1)} fusion(bf16[47,96,16,32]{1,3,0,2:T(8,128)(2,1)S(1)} %fusion.122, bf16[47,96,768]{2,0,1:T(8,128)(2,1)} %get-tuple-element.5), kind=kOutput, calls=%fused_computation.77 | convolution fusion | flops 3548381184 | bytes 13123584 | tf_op jit(solution)/shard_map/lrc,lrn->cn/dot_general | solution.py:55
  492.7 6.2 fusion.64
  498.9 1.9 pad_maximum_fusion
  500.8 138.4 %reduce-scatter.2.cloned.1.call-done = f32[2,768,32]{1,2,0:T(8,128)} async-done(((f32[32,768,32]{1,2,0:T(8,128)}), f32[2,768,32]{1,2,0:T(8,128)}) %reduce-scatter.2.cloned.1.call-update) | async-done | bytes 196624 | tf_op jit(solution)/shard_map/reduce_scatter | solution.py:96
  640.5 67.7 %all-gather = f32[1024,32]{1,0:T(8,128)S(1)} all-gather(f32[32,32]{1,0:T(8,128)S(1)} %convolution_bitcast_fusion.1), channel_id=2, replica_groups=mesh['row'=16,'col'=2] {'row','col'}, dimensions={0}, use_global_device_ids=true | all-gather | bytes 135168 | tf_op jit(solution)/shard_map/all_gather | solution.py:98
  714.9 1.9 convolution_multiply_fusion
  (70 shorter events, 9.1 us)
Async XLA Ops:
  33.3 7.7 %copy-start = (s32[32]{0:T(128)S(1)}, s32[32]{0:T(128)}, u32[]{:S(2)}) copy-start(s32[32]{0:T(128)} %param.3) | copy-start | bytes 388
  33.3 340.8 %all-to-all-start = ((bf16[768,8,1536]{0,1,2:T(8,128)(2,1)}), bf16[768,8,1536]{0,1,2:T(8,128)(2,1)}, u32[]{:S(2)}, u32[]{:S(2)}) async-start(bf16[768,8,1536]{0,1,2:T(8,128)(2,1)} %copy.35), calls=%async_computation | async-start | bytes 37748736 | tf_op jit(solution)/shard_map/all_to_all | solution.py:85
  40.9 598.3 %reduce-scatter.2.cloned.1.call-start = ((), (), s32[]{:S(2)}) async-start(), calls=%async_computation.2 | async-start | bytes 3342336 | tf_op jit(solution)/shard_map/reduce_scatter | solution.py:96
  475.7 17.0 %slice-start = ((s8[7077888]{0:T(1024)(128)(4,1)}), s8[4194304]{0:T(1024)(128)(4,1)S(1)}, s32[]{:S(2)}) async-start(s8[7077888]{0:T(1024)(128)(4,1)} %bitcast.323), calls=%async_computation.3 | async-start | bytes 8388608
  476.2 16.5 %slice-start.1 = ((s8[7077888]{0:T(1024)(128)(4,1)}), s8[2883584]{0:T(1024)(128)(4,1)S(1)}, s32[]{:S(2)}) async-start(s8[7077888]{0:T(1024)(128)(4,1)} %bitcast.323), calls=%async_computation.4 | async-start | bytes 5767168
Sparse Core Ops, SparseCore 0:
  500.9 138.1 reduce-scatter.1
